TPU v7x, 32 devices: a whole 2x2x4 slice. The times are simulated.
32 devices in a mesh: img: 8 (over y, x, core), cls: 4 (over z).
Axes of the slice: x: 2, y: 2, z: 4, core: 2. Of those that a mesh axis runs over, the one named last changes fastest.
Arguments:
- images: bfloat16 [64, 9216], P('img'), may hold values from -64 to 64
- references: bfloat16 [512, 9216], P(('img', 'cls')), may hold values from -0.2 to 0.2
- class_logprior: bfloat16 [512], P(('img', 'cls')), may hold values from -3 to 3
- ctf_table: float32 [16, 32], replicated, may hold values from -1 to 1, as said below
- noise_power: float32 [32], replicated, may hold values from 0.5 to 2
- tau_power: float32 [32], replicated, may hold values from 0.5 to 4
- defocus: int32 [64], P('img'), may hold values from 0 to 15
- offsets: int32 [64, 4, 2], P('img'), may hold values from -3 to 3
Outputs:
- new_refs: float32 [512, 9216], P(('img', 'cls'))
- new_weights: float32 [512], P(('img', 'cls'))
- loglik: float32 [64], P('img')
Inputs may be any that keep to these rules, and one draw needn't show every extreme that they name: `ctf_table`: each row is a contrast transfer curve that oscillates over the cycles.
All inputs are finite; a program needn't handle non-finite values.
Results may differ from a plain program's by a relative error of at most 0.0068.
Values may be sent and summed in bfloat16 or wider, within the bound.
A program may use at most 64 MiB of HBM per device.

v0:
```python
import math

import jax
import jax.numpy as jnp
from jax import lax
from jax.sharding import PartitionSpec as P

TRANS = 4
CYCLES = 32
ANG = 144
ROT = 36
NDEF = 16


offset_sigma = 2.0
turn_group = 4


def phase_table(shift_x, shift_y):
    radius = jnp.arange(CYCLES, dtype=jnp.float32) + 1.0
    theta = 2.0 * math.pi * jnp.arange(ANG, dtype=jnp.float32) / ANG
    freq_x = radius[:, None] * jnp.cos(theta)[None, :]
    freq_y = radius[:, None] * jnp.sin(theta)[None, :]
    return (
        -2.0
        * math.pi
        * (shift_x[..., None, None] * freq_x + shift_y[..., None, None] * freq_y)
        / (2.0 * CYCLES)
    )


def turned_rows(source, group_index, stride):
    shaped = source.reshape(source.shape[0], 2, CYCLES, ANG)
    first_turn = group_index * turn_group
    turned = [
        jnp.roll(shaped, -stride * (first_turn + step), axis=-1) for step in range(turn_group)
    ]
    return jnp.stack(turned, axis=1).reshape(source.shape[0] * turn_group, source.shape[1])


def per_device(
    images, references, class_logprior, ctf_table, noise_power, tau_power, defocus, offsets
):
    img_count = images.shape[0]
    rows = img_count * TRANS
    width = images.shape[1]
    stride = ANG // ROT
    owned = references.shape[0]
    classes = owned * lax.axis_size("img")
    groups_count = ROT // turn_group
    pixels = images.astype(jnp.float32).reshape(img_count, 2, CYCLES, ANG)
    shift = offsets.astype(jnp.float32)
    angle = phase_table(shift[..., 0], shift[..., 1])
    cosine = jnp.cos(angle)
    sine = jnp.sin(angle)
    real_part = pixels[:, None, 0] * cosine - pixels[:, None, 1] * sine
    imag_part = pixels[:, None, 0] * sine + pixels[:, None, 1] * cosine
    shifted = jnp.stack([real_part, imag_part], axis=2)
    one_hot = (defocus[:, None] == jnp.arange(NDEF, dtype=jnp.int32)[None, :]).astype(jnp.float32)
    contrast = jnp.dot(one_hot, ctf_table, precision=lax.Precision.HIGHEST)
    weighted = (
        (shifted * (contrast / noise_power[None, :])[:, None, None, :, None])
        .astype(jnp.bfloat16)
        .reshape(rows, width)
    )
    inserted = (
        (shifted * contrast[:, None, None, :, None]).astype(jnp.bfloat16).reshape(rows, width)
    )
    norm_coef = jnp.repeat(contrast * contrast / (2.0 * noise_power[None, :]), TRANS, axis=0)
    squared_rows = jnp.repeat(contrast * contrast, TRANS, axis=0)
    trans_prior = -(shift[..., 0] * shift[..., 0] + shift[..., 1] * shift[..., 1]) / (
        2.0 * offset_sigma * offset_sigma
    )
    group_refs, group_prior = (
        lax.all_gather(references, "img", axis=0, tiled=True),
        lax.all_gather(class_logprior, "img", axis=0, tiled=True),
    )
    power = jnp.sum(
        jnp.square(group_refs.astype(jnp.float32).reshape(classes, 2, CYCLES, ANG)), axis=(1, 3)
    )
    penalty = jnp.dot(norm_coef, power.T, precision=lax.Precision.HIGHEST)
    base_scores = (
        group_prior.astype(jnp.float32)[None, :] - penalty + trans_prior.reshape(rows)[:, None]
    )

    def score_group(group_index, current):
        rotated = turned_rows(weighted, group_index, stride)
        cross = lax.dot_general(
            rotated, group_refs, (((1,), (1,)), ((), ())), preferred_element_type=jnp.float32
        )
        values = cross.reshape(rows, turn_group, classes) + base_scores[:, None, :]
        return lax.dynamic_update_slice_in_dim(current, values, group_index * turn_group, 1)

    logp = lax.fori_loop(0, groups_count, score_group, jnp.zeros((rows, ROT, classes), jnp.float32))
    per_image = logp.reshape(img_count, TRANS * ROT * classes)
    local_peak = jnp.max(per_image, axis=1)
    peak = lax.pmax(local_peak, "cls")
    total = lax.psum(jnp.sum(jnp.exp(per_image - peak[:, None]), axis=1), "cls")
    loglik = peak + jnp.log(total)
    posterior = (
        (jnp.exp(per_image - peak[:, None]) / total[:, None])
        .astype(jnp.bfloat16)
        .reshape(rows, ROT, classes)
    )

    def insert_group(group_index, numer):
        rotated = turned_rows(inserted, group_index, stride)
        section = lax.dynamic_slice_in_dim(
            posterior, group_index * turn_group, turn_group, 1
        ).reshape(rows * turn_group, classes)
        return numer + lax.dot_general(
            section, rotated, (((0,), (0,)), ((), ())), preferred_element_type=jnp.float32
        )

    numer = lax.fori_loop(0, groups_count, insert_group, jnp.zeros((classes, width), jnp.float32))
    post_sum = jnp.sum(posterior.astype(jnp.float32), axis=1)
    denom = lax.dot_general(
        post_sum, squared_rows, (((0,), (0,)), ((), ())), precision=lax.Precision.HIGHEST
    )
    weight = jnp.sum(post_sum, axis=0)
    numer_own, denom_own, weight_own = (
        lax.psum_scatter(numer, "img", scatter_dimension=0, tiled=True),
        lax.psum_scatter(denom, "img", scatter_dimension=0, tiled=True),
        lax.psum_scatter(weight, "img", scatter_dimension=0, tiled=True),
    )
    fresh = numer_own.reshape(owned, 2, CYCLES, ANG) / (
        denom_own[:, None, :, None] + 1.0 / tau_power[None, None, :, None]
    )
    return (fresh.reshape(owned, width), weight_own / (img_count * lax.axis_size("img")), loglik)


def solution(mesh):
    return jax.shard_map(
        per_device,
        mesh=mesh,
        in_specs=(
            P("img", None),
            P(("img", "cls"), None),
            P(("img", "cls")),
            P(),
            P(),
            P(),
            P("img"),
            P("img", None, None),
        ),
        out_specs=(P(("img", "cls"), None), P(("img", "cls")), P("img")),
        check_vma=False,
    )
```

profile of v0, /device:TPU:0, one launch (start us, length us, event | category | flops | bytes accessed | tf_op | source)
XLA Modules:
  0.0 554.3 jit_solution(16485100970183004758)
XLA Ops:
  13.2 15.3 %all-reduce = bf16[128]{0:T(256)(128)(2,1)S(1)} all-reduce(bf16[128]{0:T(256)(128)(2,1)S(1)} %dynamic-update-slice), channel_id=1, replica_groups=mesh['img'=8,'cls'=4] {'img'}, use_global_device_ids=true, to_apply=%add | all-reduce | flops 128 | bytes 512
  30.2 4.1 multiply_subtract_fusion
  35.6 6.0 %all-gather.2.cloned.1.call-done = bf16[128,9216]{1,0:T(8,128)(2,1)} async-done(((bf16[16,9216]{1,0:T(8,128)(2,1)}), bf16[128,9216]{1,0:T(8,128)(2,1)}) %all-gather.2.cloned.1.call-update) | async-done | bytes 2359312 | tf_op jit(solution)/shard_map/all_gather | solution.py:75
  41.6 3.0 copy.37
  50.6 221.6 %while.31 = (s32[]{:T(128)}, f32[32,36,128]{2,0,1:T(8,128)}, bf16[8,4,2,32,144]{4,3,2,1,0:T(8,128)(2,1)S(1)}, bf16[128,9216]{1,0:T(8,128)(2,1)}, f32[32,128]{1,0...) while((s32[]{:T(128)}, f32[32,36,128]{2,0,1:T(8,128)}, ...), condition=%wide.region_2.4_spmd, body=%wide.region_1.3_spmd.sunk | while | flops 310263872 | bytes 21906228 | solution.py:94
  51.6 10.1 %fusion.59 = (bf16[32,2,32,144]{3,2,1,0:T(8,128)(2,1)S(1)}, bf16[32,2,32,144]{3,2,1,0:T(8,128)(2,1)S(1)}, bf16[32,2,32,144]{3,2,1,0:T(8,128)(2,1)S(1)}, bf16[32,2,32,144]{3,2,1,0:T(8,128)(2,1)}) fusion(s32[]{:T(128)S(6)} %select_n.81, bf16[32,2,32,144]{3,2,1,0:T(8,128)(2,1)} %bitcast.71, s32[]{:T(128)S(6)} %select_n.83, s32[]{:T(128)S(6)} %select_n.85, ...), kind=kLoop, calls=%fused_computation.20.clone.1 | loop fusion | flops 4718592 | bytes 2949136 | tf_op jit(solution)/shard_map/while/body/eval_jaxpr/jit(_roll_dynamic)/concatenate | solution.py:36
  61.7 3.3 stack.105
  71.7 3.4 fusion.60
  76.1 10.3 %fusion.59 = (bf16[32,2,32,144]{3,2,1,0:T(8,128)(2,1)S(1)}, bf16[32,2,32,144]{3,2,1,0:T(8,128)(2,1)S(1)}, bf16[32,2,32,144]{3,2,1,0:T(8,128)(2,1)S(1)}, bf16[32,2,32,144]{3,2,1,0:T(8,128)(2,1)}) fusion(s32[]{:T(128)S(6)} %select_n.81, bf16[32,2,32,144]{3,2,1,0:T(8,128)(2,1)} %bitcast.71, s32[]{:T(128)S(6)} %select_n.83, s32[]{:T(128)S(6)} %select_n.85, ...), kind=kLoop, calls=%fused_computation.20.clone.1 | loop fusion | flops 4718592 | bytes 2949136 | tf_op jit(solution)/shard_map/while/body/eval_jaxpr/jit(_roll_dynamic)/concatenate | solution.py:36
  86.4 3.3 stack.105
  96.5 3.4 fusion.60
  100.8 10.3 %fusion.59 = (bf16[32,2,32,144]{3,2,1,0:T(8,128)(2,1)S(1)}, bf16[32,2,32,144]{3,2,1,0:T(8,128)(2,1)S(1)}, bf16[32,2,32,144]{3,2,1,0:T(8,128)(2,1)S(1)}, bf16[32,2,32,144]{3,2,1,0:T(8,128)(2,1)}) fusion(s32[]{:T(128)S(6)} %select_n.81, bf16[32,2,32,144]{3,2,1,0:T(8,128)(2,1)} %bitcast.71, s32[]{:T(128)S(6)} %select_n.83, s32[]{:T(128)S(6)} %select_n.85, ...), kind=kLoop, calls=%fused_computation.20.clone.1 | loop fusion | flops 4718592 | bytes 2949136 | tf_op jit(solution)/shard_map/while/body/eval_jaxpr/jit(_roll_dynamic)/concatenate | solution.py:36
  111.1 3.3 stack.105
  121.2 3.4 fusion.60
  125.6 10.3 %fusion.59 = (bf16[32,2,32,144]{3,2,1,0:T(8,128)(2,1)S(1)}, bf16[32,2,32,144]{3,2,1,0:T(8,128)(2,1)S(1)}, bf16[32,2,32,144]{3,2,1,0:T(8,128)(2,1)S(1)}, bf16[32,2,32,144]{3,2,1,0:T(8,128)(2,1)}) fusion(s32[]{:T(128)S(6)} %select_n.81, bf16[32,2,32,144]{3,2,1,0:T(8,128)(2,1)} %bitcast.71, s32[]{:T(128)S(6)} %select_n.83, s32[]{:T(128)S(6)} %select_n.85, ...), kind=kLoop, calls=%fused_computation.20.clone.1 | loop fusion | flops 4718592 | bytes 2949136 | tf_op jit(solution)/shard_map/while/body/eval_jaxpr/jit(_roll_dynamic)/concatenate | solution.py:36
  135.9 3.3 stack.105
  145.9 3.4 fusion.60
  150.3 10.3 %fusion.59 = (bf16[32,2,32,144]{3,2,1,0:T(8,128)(2,1)S(1)}, bf16[32,2,32,144]{3,2,1,0:T(8,128)(2,1)S(1)}, bf16[32,2,32,144]{3,2,1,0:T(8,128)(2,1)S(1)}, bf16[32,2,32,144]{3,2,1,0:T(8,128)(2,1)}) fusion(s32[]{:T(128)S(6)} %select_n.81, bf16[32,2,32,144]{3,2,1,0:T(8,128)(2,1)} %bitcast.71, s32[]{:T(128)S(6)} %select_n.83, s32[]{:T(128)S(6)} %select_n.85, ...), kind=kLoop, calls=%fused_computation.20.clone.1 | loop fusion | flops 4718592 | bytes 2949136 | tf_op jit(solution)/shard_map/while/body/eval_jaxpr/jit(_roll_dynamic)/concatenate | solution.py:36
  160.6 3.3 stack.105
  170.6 3.4 fusion.60
  175.0 10.3 %fusion.59 = (bf16[32,2,32,144]{3,2,1,0:T(8,128)(2,1)S(1)}, bf16[32,2,32,144]{3,2,1,0:T(8,128)(2,1)S(1)}, bf16[32,2,32,144]{3,2,1,0:T(8,128)(2,1)S(1)}, bf16[32,2,32,144]{3,2,1,0:T(8,128)(2,1)}) fusion(s32[]{:T(128)S(6)} %select_n.81, bf16[32,2,32,144]{3,2,1,0:T(8,128)(2,1)} %bitcast.71, s32[]{:T(128)S(6)} %select_n.83, s32[]{:T(128)S(6)} %select_n.85, ...), kind=kLoop, calls=%fused_computation.20.clone.1 | loop fusion | flops 4718592 | bytes 2949136 | tf_op jit(solution)/shard_map/while/body/eval_jaxpr/jit(_roll_dynamic)/concatenate | solution.py:36
  185.3 3.3 stack.105
  195.4 3.4 fusion.60
  199.7 10.3 %fusion.59 = (bf16[32,2,32,144]{3,2,1,0:T(8,128)(2,1)S(1)}, bf16[32,2,32,144]{3,2,1,0:T(8,128)(2,1)S(1)}, bf16[32,2,32,144]{3,2,1,0:T(8,128)(2,1)S(1)}, bf16[32,2,32,144]{3,2,1,0:T(8,128)(2,1)}) fusion(s32[]{:T(128)S(6)} %select_n.81, bf16[32,2,32,144]{3,2,1,0:T(8,128)(2,1)} %bitcast.71, s32[]{:T(128)S(6)} %select_n.83, s32[]{:T(128)S(6)} %select_n.85, ...), kind=kLoop, calls=%fused_computation.20.clone.1 | loop fusion | flops 4718592 | bytes 2949136 | tf_op jit(solution)/shard_map/while/body/eval_jaxpr/jit(_roll_dynamic)/concatenate | solution.py:36
  210.0 3.3 stack.105
  220.1 3.4 fusion.60
  224.5 10.3 %fusion.59 = (bf16[32,2,32,144]{3,2,1,0:T(8,128)(2,1)S(1)}, bf16[32,2,32,144]{3,2,1,0:T(8,128)(2,1)S(1)}, bf16[32,2,32,144]{3,2,1,0:T(8,128)(2,1)S(1)}, bf16[32,2,32,144]{3,2,1,0:T(8,128)(2,1)}) fusion(s32[]{:T(128)S(6)} %select_n.81, bf16[32,2,32,144]{3,2,1,0:T(8,128)(2,1)} %bitcast.71, s32[]{:T(128)S(6)} %select_n.83, s32[]{:T(128)S(6)} %select_n.85, ...), kind=kLoop, calls=%fused_computation.20.clone.1 | loop fusion | flops 4718592 | bytes 2949136 | tf_op jit(solution)/shard_map/while/body/eval_jaxpr/jit(_roll_dynamic)/concatenate | solution.py:36
  234.8 3.3 stack.105
  244.8 3.4 fusion.60
  249.2 9.6 %fusion.59 = (bf16[32,2,32,144]{3,2,1,0:T(8,128)(2,1)S(1)}, bf16[32,2,32,144]{3,2,1,0:T(8,128)(2,1)S(1)}, bf16[32,2,32,144]{3,2,1,0:T(8,128)(2,1)S(1)}, bf16[32,2,32,144]{3,2,1,0:T(8,128)(2,1)}) fusion(s32[]{:T(128)S(6)} %select_n.81, bf16[32,2,32,144]{3,2,1,0:T(8,128)(2,1)} %bitcast.71, s32[]{:T(128)S(6)} %select_n.83, s32[]{:T(128)S(6)} %select_n.85, ...), kind=kLoop, calls=%fused_computation.20.clone.1 | loop fusion | flops 4718592 | bytes 2949136 | tf_op jit(solution)/shard_map/while/body/eval_jaxpr/jit(_roll_dynamic)/concatenate | solution.py:36
  258.8 3.3 stack.105
  268.8 3.4 fusion.60
  273.7 11.7 %pmax.7 = f32[8]{0:T(128)S(1)} all-reduce(f32[8]{0:T(128)S(1)} %reduce_max.18), channel_id=1, replica_groups=mesh['img'=8,'cls'=4] {'cls'}, use_global_device_ids=true, to_apply=%region_5.7 | all-reduce | flops 8 | bytes 64 | tf_op jit(solution)/shard_map/pmax | solution.py:97
  287.4 8.6 %psum.7 = f32[8]{0:T(128)S(1)} all-reduce(f32[8]{0:T(128)S(1)} %reduce_sum.46), channel_id=1, replica_groups=mesh['img'=8,'cls'=4] {'cls'}, use_global_device_ids=true, to_apply=%region_8.10 | all-reduce | flops 8 | bytes 64 | tf_op jit(solution)/shard_map/psum | solution.py:98
  299.5 193.8 %while.32 = (s32[]{:T(128)}, f32[128,9216]{1,0:T(8,128)}, bf16[32,36,128]{2,1,0:T(8,128)(2,1)}, bf16[8,4,2,32,144]{4,3,2,1,0:T(8,128)(2,1)S(1)}, s32[]{:T(128)},...) while((s32[]{:T(128)}, f32[128,9216]{1,0:T(8,128)}, ...), condition=%wide.region_10.12_spmd.clone, body=%wide.region_9.11_spmd.clone.sunk | while | flops 312606784 | bytes 24281796 | solution.py:115
  299.6 5.7 %fusion.63 = (bf16[32,1,2,32,144]{4,3,2,1,0:T(8,128)(2,1)S(1)}, bf16[32,1,2,32,144]{4,3,2,1,0:T(8,128)(2,1)S(1)}, bf16[32,1,2,32,144]{4,3,2,1,0:T(8,128)(2,1)S(1)}, bf16[32,1,2,32,144]{4,3,2,1,0:T(8,128)(2,1)S(1)}) fusion(s32[]{:T(128)S(6)} %select_n.90, bf16[32,2,32,144]{3,2,1,0:T(8,128)(2,1)S(1)} %bitcast.70, s32[]{:T(128)S(6)} %select_n.92, ...), kind=kLoop, calls=%fused_computation.37.clone.1 | loop fusion | flops 4718592 | bytes 2949136 | tf_op jit(solution)/shard_map/while/body/eval_jaxpr/stack | solution.py:38
  307.8 7.4 %reshape.232 = bf16[128,9216]{1,0:T(8,128)(2,1)S(1)} reshape(bf16[32,4,2,32,144]{4,3,2,1,0:T(8,128)(2,1)} %pad_maximum_fusion.3) | data formatting | bytes 4718592 | tf_op jit(solution)/shard_map/while/body/eval_jaxpr/reshape | solution.py:38
  316.1 3.0 convolution_add_fusion.2
  319.1 5.7 %fusion.63 = (bf16[32,1,2,32,144]{4,3,2,1,0:T(8,128)(2,1)S(1)}, bf16[32,1,2,32,144]{4,3,2,1,0:T(8,128)(2,1)S(1)}, bf16[32,1,2,32,144]{4,3,2,1,0:T(8,128)(2,1)S(1)}, bf16[32,1,2,32,144]{4,3,2,1,0:T(8,128)(2,1)S(1)}) fusion(s32[]{:T(128)S(6)} %select_n.90, bf16[32,2,32,144]{3,2,1,0:T(8,128)(2,1)S(1)} %bitcast.70, s32[]{:T(128)S(6)} %select_n.92, ...), kind=kLoop, calls=%fused_computation.37.clone.1 | loop fusion | flops 4718592 | bytes 2949136 | tf_op jit(solution)/shard_map/while/body/eval_jaxpr/stack | solution.py:38
  327.3 7.4 %reshape.232 = bf16[128,9216]{1,0:T(8,128)(2,1)S(1)} reshape(bf16[32,4,2,32,144]{4,3,2,1,0:T(8,128)(2,1)} %pad_maximum_fusion.3) | data formatting | bytes 4718592 | tf_op jit(solution)/shard_map/while/body/eval_jaxpr/reshape | solution.py:38
  335.6 5.3 convolution_add_fusion.2
  340.9 5.7 %fusion.63 = (bf16[32,1,2,32,144]{4,3,2,1,0:T(8,128)(2,1)S(1)}, bf16[32,1,2,32,144]{4,3,2,1,0:T(8,128)(2,1)S(1)}, bf16[32,1,2,32,144]{4,3,2,1,0:T(8,128)(2,1)S(1)}, bf16[32,1,2,32,144]{4,3,2,1,0:T(8,128)(2,1)S(1)}) fusion(s32[]{:T(128)S(6)} %select_n.90, bf16[32,2,32,144]{3,2,1,0:T(8,128)(2,1)S(1)} %bitcast.70, s32[]{:T(128)S(6)} %select_n.92, ...), kind=kLoop, calls=%fused_computation.37.clone.1 | loop fusion | flops 4718592 | bytes 2949136 | tf_op jit(solution)/shard_map/while/body/eval_jaxpr/stack | solution.py:38
  349.1 7.4 %reshape.232 = bf16[128,9216]{1,0:T(8,128)(2,1)S(1)} reshape(bf16[32,4,2,32,144]{4,3,2,1,0:T(8,128)(2,1)} %pad_maximum_fusion.3) | data formatting | bytes 4718592 | tf_op jit(solution)/shard_map/while/body/eval_jaxpr/reshape | solution.py:38
  357.3 5.3 convolution_add_fusion.2
  362.7 5.7 %fusion.63 = (bf16[32,1,2,32,144]{4,3,2,1,0:T(8,128)(2,1)S(1)}, bf16[32,1,2,32,144]{4,3,2,1,0:T(8,128)(2,1)S(1)}, bf16[32,1,2,32,144]{4,3,2,1,0:T(8,128)(2,1)S(1)}, bf16[32,1,2,32,144]{4,3,2,1,0:T(8,128)(2,1)S(1)}) fusion(s32[]{:T(128)S(6)} %select_n.90, bf16[32,2,32,144]{3,2,1,0:T(8,128)(2,1)S(1)} %bitcast.70, s32[]{:T(128)S(6)} %select_n.92, ...), kind=kLoop, calls=%fused_computation.37.clone.1 | loop fusion | flops 4718592 | bytes 2949136 | tf_op jit(solution)/shard_map/while/body/eval_jaxpr/stack | solution.py:38
  370.8 7.4 %reshape.232 = bf16[128,9216]{1,0:T(8,128)(2,1)S(1)} reshape(bf16[32,4,2,32,144]{4,3,2,1,0:T(8,128)(2,1)} %pad_maximum_fusion.3) | data formatting | bytes 4718592 | tf_op jit(solution)/shard_map/while/body/eval_jaxpr/reshape | solution.py:38
  379.1 5.3 convolution_add_fusion.2
  384.5 5.7 %fusion.63 = (bf16[32,1,2,32,144]{4,3,2,1,0:T(8,128)(2,1)S(1)}, bf16[32,1,2,32,144]{4,3,2,1,0:T(8,128)(2,1)S(1)}, bf16[32,1,2,32,144]{4,3,2,1,0:T(8,128)(2,1)S(1)}, bf16[32,1,2,32,144]{4,3,2,1,0:T(8,128)(2,1)S(1)}) fusion(s32[]{:T(128)S(6)} %select_n.90, bf16[32,2,32,144]{3,2,1,0:T(8,128)(2,1)S(1)} %bitcast.70, s32[]{:T(128)S(6)} %select_n.92, ...), kind=kLoop, calls=%fused_computation.37.clone.1 | loop fusion | flops 4718592 | bytes 2949136 | tf_op jit(solution)/shard_map/while/body/eval_jaxpr/stack | solution.py:38
  392.6 7.4 %reshape.232 = bf16[128,9216]{1,0:T(8,128)(2,1)S(1)} reshape(bf16[32,4,2,32,144]{4,3,2,1,0:T(8,128)(2,1)} %pad_maximum_fusion.3) | data formatting | bytes 4718592 | tf_op jit(solution)/shard_map/while/body/eval_jaxpr/reshape | solution.py:38
  400.9 5.3 convolution_add_fusion.2
  406.2 5.7 %fusion.63 = (bf16[32,1,2,32,144]{4,3,2,1,0:T(8,128)(2,1)S(1)}, bf16[32,1,2,32,144]{4,3,2,1,0:T(8,128)(2,1)S(1)}, bf16[32,1,2,32,144]{4,3,2,1,0:T(8,128)(2,1)S(1)}, bf16[32,1,2,32,144]{4,3,2,1,0:T(8,128)(2,1)S(1)}) fusion(s32[]{:T(128)S(6)} %select_n.90, bf16[32,2,32,144]{3,2,1,0:T(8,128)(2,1)S(1)} %bitcast.70, s32[]{:T(128)S(6)} %select_n.92, ...), kind=kLoop, calls=%fused_computation.37.clone.1 | loop fusion | flops 4718592 | bytes 2949136 | tf_op jit(solution)/shard_map/while/body/eval_jaxpr/stack | solution.py:38
  414.4 7.4 %reshape.232 = bf16[128,9216]{1,0:T(8,128)(2,1)S(1)} reshape(bf16[32,4,2,32,144]{4,3,2,1,0:T(8,128)(2,1)} %pad_maximum_fusion.3) | data formatting | bytes 4718592 | tf_op jit(solution)/shard_map/while/body/eval_jaxpr/reshape | solution.py:38
  422.7 5.3 convolution_add_fusion.2
  428.0 5.7 %fusion.63 = (bf16[32,1,2,32,144]{4,3,2,1,0:T(8,128)(2,1)S(1)}, bf16[32,1,2,32,144]{4,3,2,1,0:T(8,128)(2,1)S(1)}, bf16[32,1,2,32,144]{4,3,2,1,0:T(8,128)(2,1)S(1)}, bf16[32,1,2,32,144]{4,3,2,1,0:T(8,128)(2,1)S(1)}) fusion(s32[]{:T(128)S(6)} %select_n.90, bf16[32,2,32,144]{3,2,1,0:T(8,128)(2,1)S(1)} %bitcast.70, s32[]{:T(128)S(6)} %select_n.92, ...), kind=kLoop, calls=%fused_computation.37.clone.1 | loop fusion | flops 4718592 | bytes 2949136 | tf_op jit(solution)/shard_map/while/body/eval_jaxpr/stack | solution.py:38
  436.2 7.4 %reshape.232 = bf16[128,9216]{1,0:T(8,128)(2,1)S(1)} reshape(bf16[32,4,2,32,144]{4,3,2,1,0:T(8,128)(2,1)} %pad_maximum_fusion.3) | data formatting | bytes 4718592 | tf_op jit(solution)/shard_map/while/body/eval_jaxpr/reshape | solution.py:38
  444.5 5.3 convolution_add_fusion.2
  449.8 5.7 %fusion.63 = (bf16[32,1,2,32,144]{4,3,2,1,0:T(8,128)(2,1)S(1)}, bf16[32,1,2,32,144]{4,3,2,1,0:T(8,128)(2,1)S(1)}, bf16[32,1,2,32,144]{4,3,2,1,0:T(8,128)(2,1)S(1)}, bf16[32,1,2,32,144]{4,3,2,1,0:T(8,128)(2,1)S(1)}) fusion(s32[]{:T(128)S(6)} %select_n.90, bf16[32,2,32,144]{3,2,1,0:T(8,128)(2,1)S(1)} %bitcast.70, s32[]{:T(128)S(6)} %select_n.92, ...), kind=kLoop, calls=%fused_computation.37.clone.1 | loop fusion | flops 4718592 | bytes 2949136 | tf_op jit(solution)/shard_map/while/body/eval_jaxpr/stack | solution.py:38
  458.0 7.4 %reshape.232 = bf16[128,9216]{1,0:T(8,128)(2,1)S(1)} reshape(bf16[32,4,2,32,144]{4,3,2,1,0:T(8,128)(2,1)} %pad_maximum_fusion.3) | data formatting | bytes 4718592 | tf_op jit(solution)/shard_map/while/body/eval_jaxpr/reshape | solution.py:38
  466.2 5.3 convolution_add_fusion.2
  471.6 5.7 %fusion.63 = (bf16[32,1,2,32,144]{4,3,2,1,0:T(8,128)(2,1)S(1)}, bf16[32,1,2,32,144]{4,3,2,1,0:T(8,128)(2,1)S(1)}, bf16[32,1,2,32,144]{4,3,2,1,0:T(8,128)(2,1)S(1)}, bf16[32,1,2,32,144]{4,3,2,1,0:T(8,128)(2,1)S(1)}) fusion(s32[]{:T(128)S(6)} %select_n.90, bf16[32,2,32,144]{3,2,1,0:T(8,128)(2,1)S(1)} %bitcast.70, s32[]{:T(128)S(6)} %select_n.92, ...), kind=kLoop, calls=%fused_computation.37.clone.1 | loop fusion | flops 4718592 | bytes 2949136 | tf_op jit(solution)/shard_map/while/body/eval_jaxpr/stack | solution.py:38
  479.7 7.4 %reshape.232 = bf16[128,9216]{1,0:T(8,128)(2,1)S(1)} reshape(bf16[32,4,2,32,144]{4,3,2,1,0:T(8,128)(2,1)} %pad_maximum_fusion.3) | data formatting | bytes 4718592 | tf_op jit(solution)/shard_map/while/body/eval_jaxpr/reshape | solution.py:38
  488.0 5.3 convolution_add_fusion.2
  494.0 11.8 %all-reduce.1 = f32[128]{0:T(128)S(1)} all-reduce(f32[128]{0:T(128)S(1)} %get-tuple-element.268), channel_id=4, replica_groups=mesh['img'=8,'cls'=4] {'img'}, use_global_device_ids=true, to_apply=%region_15.17.clone | all-reduce | flops 128 | bytes 1024
  508.3 37.4 %reduce-scatter.3.cloned.1.call-done = f32[16,9216]{1,0:T(8,128)} async-done(((f32[128,9216]{1,0:T(8,128)}), f32[16,9216]{1,0:T(8,128)}) %reduce-scatter.3.cloned.1.call-update) | async-done | bytes 589840 | tf_op jit(solution)/shard_map/reduce_scatter | solution.py:122
  (174 shorter events, 125.1 us)
Async XLA Ops:
  7.2 22.0 %copy-start = (f32[16,32]{1,0:T(8,128)S(1)}, f32[16,32]{1,0:T(8,128)}, u32[]{:S(2)}) copy-start(f32[16,32]{1,0:T(8,128)} %param.17) | copy-start | bytes 6148
  7.2 34.4 %all-gather.2.cloned.1.call-start = ((), (), s32[]{:S(2)}) async-start(), calls=%async_computation.2 | async-start | bytes 2654208 | tf_op jit(solution)/shard_map/all_gather | solution.py:75
  7.9 499.1 %reduce-scatter.5.cloned.1.call-start = ((), (), s32[]{:S(2)}) async-start(), calls=%async_computation.4 | async-start | bytes 73728 | tf_op jit(solution)/shard_map/reduce_scatter | solution.py:123
  50.6 1.0 copy-start.2
  67.5 4.2 copy-start.4
  67.5 4.2 copy-start.5
  71.7 3.4 copy-start.3
  75.1 1.0 copy-start.2
  92.2 4.2 copy-start.4
  92.2 4.2 copy-start.5
  96.5 3.4 copy-start.3
  99.9 1.0 copy-start.2
  117.0 4.2 copy-start.4
  117.0 4.2 copy-start.5
  121.2 3.4 copy-start.3
  124.6 1.0 copy-start.2
  141.7 4.2 copy-start.4
  141.7 4.2 copy-start.5
  145.9 3.4 copy-start.3
  149.3 1.0 copy-start.2
  166.4 4.2 copy-start.4
  166.4 4.2 copy-start.5
  170.6 3.4 copy-start.3
  174.0 1.0 copy-start.2
  191.1 4.2 copy-start.4
  191.1 4.2 copy-start.5
  195.4 3.4 copy-start.3
  198.7 1.0 copy-start.2
  215.8 4.2 copy-start.4
  215.9 4.2 copy-start.5
  220.1 3.4 copy-start.3
  223.5 1.0 copy-start.2
  240.6 4.2 copy-start.4
  240.6 4.2 copy-start.5
  244.8 3.4 copy-start.3
  248.2 1.0 copy-start.2
  264.6 4.2 copy-start.4
  264.6 4.2 copy-start.5
  268.8 3.4 copy-start.3
  272.2 27.3 %copy-start.1 = (bf16[8,4,2,32,144]{4,3,2,1,0:T(8,128)(2,1)S(1)}, bf16[8,4,2,32,144]{4,3,2,1,0:T(8,128)(2,1)}, u32[]{:S(2)}) copy-start(bf16[8,4,2,32,144]{4,3,2,1,0:T(8,128)(2,1)} %get-tuple-element.436) | copy-start | bytes 1769476
  299.4 246.3 %reduce-scatter.3.cloned.1.call-start = ((), (), s32[]{:S(2)}) async-start(), calls=%async_computation.3 | async-start | bytes 5308416 | tf_op jit(solution)/shard_map/reduce_scatter | solution.py:122
  493.4 0.7 copy-start.6
Sparse Core Ops, SparseCore 0:
  9.9 31.6 all-gather.1
  299.6 31.9 reduce-scatter.4
  493.5 52.2 reduce-scatter.2
where the time goes:
time: 557 us; the launch traced here: 554 us
  other arithmetic  186 us (33%)
  local copies, waits for them, and re-layouts  182 us (33%)
  matrix products  78.1 us (14%)
  blocking collectives  47.4 us (9%)
  waiting for transfers between devices  44.1 us (8%)
  between operations  15.2 us (3%)
    concatenate x9, other arithmetic, turned_rows(): jnp.roll(shaped, -stride * (first_turn + step), axis=-1)  91.8 us
    another operation x36, local copies, waits for them, and re-layouts, turned_rows(): jnp.stack(turned, axis=1)  90 us
    another operation x18, other arithmetic, turned_rows(): jnp.stack(turned, axis=1)  73.5 us
    reshape x9, local copies, waits for them, and re-layouts, turned_rows(): jnp.stack(turned, axis=1)  66.4 us
    dot_general x9, matrix products, insert_group(): lax.dot_general(section, rotated, (((0,), (0,)), ((), ())), preferred_ele...  45.7 us
    reduce_scatter x1, waiting for transfers between devices, per_device(): lax.psum_scatter(numer, 'img', scatter_dimension=0, tiled=True)  37.4 us
    dot_general x9, matrix products, score_group(): lax.dot_general(rotated, group_refs, (((1,), (1,)), ((), ())), preferred_...  30.4 us
    unnamed x2, blocking collectives  27.1 us
  transfers between devices with their start and end apart: 3, of which 2 were waited for; matrix products, arithmetic and copies ran while one was open for 37% of the time, Pallas kernels for 0%

commit v1 on v0

v1 whole, which is shorter than its diff:
```python
import math

import jax
import jax.numpy as jnp
import numpy as np
from jax import lax
from jax.experimental import pallas as pl
from jax.experimental.pallas import tpu as pltpu
from jax.sharding import PartitionSpec as P

TRANS = 4
CYCLES = 32
ANG = 144
ROT = 36
NDEF = 16

STRIDE = ANG // ROT
HALF = STRIDE * CYCLES
LANES = 2 * HALF
REACH = 3
SIDE = 2 * REACH + 1
COMBOS = SIDE * SIDE
TABLE_ROWS = 112
BATCH = 4
HIGH = lax.Precision.HIGHEST
offset_sigma = 2.0


def phase_rows():
    turn = np.arange(ROT)[:, None, None]
    step = np.arange(STRIDE)[None, :, None]
    radius = np.arange(CYCLES)[None, None, :] + 1.0
    theta = 2.0 * math.pi * (STRIDE * turn + step) / ANG
    freq_x = (radius * np.cos(theta)).reshape(ROT, 1, HALF)
    freq_y = (radius * np.sin(theta)).reshape(ROT, 1, HALF)
    combo = np.arange(COMBOS)[None, :, None]
    dx = combo // SIDE - REACH
    dy = combo % SIDE - REACH
    angle = -2.0 * math.pi * (dx * freq_x + dy * freq_y) / (2.0 * CYCLES)
    full = np.concatenate([np.cos(angle), np.sin(angle)], axis=2)
    high = full.astype(jnp.bfloat16)
    low = (full - high.astype(np.float64)).astype(jnp.bfloat16)
    table = np.zeros((ROT, TABLE_ROWS, LANES), jnp.bfloat16)
    table[:, :COMBOS] = high
    table[:, COMBOS : 2 * COMBOS] = low
    return table


def turn_major(source):
    shaped = source.reshape(source.shape[0], 2, CYCLES, ROT, STRIDE)
    return shaped.transpose(3, 0, 1, 4, 2).reshape(ROT, source.shape[0], LANES)


def gather_kernel(n, own_ref, all_ref, send_sem, recv_sem, relay_send, relay_recv):
    me = lax.axis_index("img")
    partner = me + 1 - 2 * lax.rem(me, 2)
    peers = [lax.rem(me + 2 * hop, n) for hop in range(1, n // 2)]
    barrier = pltpu.get_barrier_semaphore()
    for peer in [partner] + peers:
        pl.semaphore_signal(
            barrier, inc=1, device_id={"img": peer}, device_id_type=pl.DeviceIdType.MESH
        )
    pl.semaphore_wait(barrier, n // 2)

    def send(src, dst, peer, left, landed):
        copy = pltpu.make_async_remote_copy(
            src_ref=src,
            dst_ref=dst,
            send_sem=left,
            recv_sem=landed,
            device_id={"img": peer},
            device_id_type=pl.DeviceIdType.MESH,
        )
        copy.start()
        return copy

    direct = [
        send(own_ref, all_ref.at[me], peer, send_sem.at[hop], recv_sem.at[hop])
        for hop, peer in enumerate(peers)
    ]
    relays = [send(own_ref, all_ref.at[me], partner, relay_send.at[0], relay_recv.at[0])]
    all_ref[me] = own_ref[...]
    for hop, copy in enumerate(direct):
        copy.wait_recv()
        source = lax.rem(me + n - 2 * (hop + 1), n)
        slot = all_ref.at[source]
        relays.append(
            send(slot, slot, partner, relay_send.at[hop + 1], relay_recv.at[hop + 1])
        )
    for copy in relays:
        copy.wait_recv()
    for copy in direct + relays:
        copy.wait_send()


def gather_images(own, n):
    return pl.pallas_call(
        lambda *refs: gather_kernel(n, *refs),
        out_shape=jax.ShapeDtypeStruct((n,) + own.shape, own.dtype),
        in_specs=[pl.BlockSpec(memory_space=pltpu.VMEM)],
        out_specs=pl.BlockSpec(memory_space=pltpu.VMEM),
        scratch_shapes=[
            pltpu.SemaphoreType.DMA((n // 2,)),
            pltpu.SemaphoreType.DMA((n // 2,)),
            pltpu.SemaphoreType.DMA((n // 2,)),
            pltpu.SemaphoreType.DMA((n // 2,)),
        ],
        compiler_params=pltpu.CompilerParams(collective_id=0, has_side_effects=True),
        name="gather_images",
    )(own)


def score_kernel(
    images_ref, refs_ref, prior_ref, ctf_ref, noise_ref, table_ref,
    ins_ref, expo_ref, stat_ref, square_ref, turned,
):
    n, _, local, _ = images_ref.shape
    owned = refs_ref.shape[1]
    count = n * local
    rows = count * TRANS
    height = ROT * owned
    for spot in range(2 * ROT):
        turned[spot * owned : (spot + 1) * owned] = refs_ref[-spot % ROT]
    meta = images_ref[:, ROT].astype(jnp.float32).reshape(count, LANES)
    group = lax.broadcasted_iota(jnp.int32, (count, NDEF), 1).astype(jnp.float32)
    chosen = (group == meta[:, :1]).astype(jnp.float32)
    contrast = jnp.dot(chosen, ctf_ref[...], precision=HIGH, preferred_element_type=jnp.float32)
    contrast = jnp.concatenate([contrast] * TRANS, axis=0)
    scaled = contrast / noise_ref[...]
    square = contrast * contrast
    square_ref[...] = square
    spot = lax.broadcasted_iota(jnp.int32, (count, TABLE_ROWS), 1).astype(jnp.float32)
    lane = lax.broadcasted_iota(jnp.int32, (count, HALF), 1)
    picks, offset_terms = [], []
    for t in range(TRANS):
        dx = meta[:, 1 + t : 2 + t]
        dy = meta[:, 1 + TRANS + t : 2 + TRANS + t]
        index = (dx + REACH) * SIDE + (dy + REACH)
        hit = (spot == index) | (spot == index + COMBOS)
        picks.append(hit.astype(jnp.float32).astype(jnp.bfloat16))
        value = -(dx * dx + dy * dy) / (2.0 * offset_sigma * offset_sigma)
        offset_terms.append(jnp.where(lane == 0, value, 0.0))
    pick = jnp.concatenate(picks, axis=0)
    offset_term = jnp.concatenate(offset_terms, axis=0)

    power = jnp.zeros((owned, HALF), jnp.float32)
    for b in range(ROT):
        entry = refs_ref[b].astype(jnp.float32)
        squares = entry * entry
        power = power + squares[:, :HALF] + squares[:, HALF:]
    by_lane = (((1,), (1,)), ((), ()))
    norm_coef = square / (2.0 * noise_ref[...])
    base = prior_ref[:, :1] - lax.dot_general(
        power, norm_coef, by_lane, precision=HIGH, preferred_element_type=jnp.float32
    )
    base = base + lax.dot_general(
        jnp.ones((owned, HALF), jnp.float32), offset_term, by_lane,
        precision=HIGH, preferred_element_type=jnp.float32,
    )

    for r in range(ROT):
        expo_ref[r * owned : (r + 1) * owned] = base

    @pl.loop(0, ROT // BATCH)
    def _(batch):
        left, right = [], []
        for part in range(BATCH):
            b = batch * BATCH + part
            phase = jnp.dot(pick, table_ref[b], preferred_element_type=jnp.float32)
            cosine, sine = phase[:, :HALF], phase[:, HALF:]
            picture = images_ref[:, b].astype(jnp.float32).reshape(count, LANES)
            picture = jnp.concatenate([picture] * TRANS, axis=0)
            real, imag = picture[:, :HALF], picture[:, HALF:]
            moved_real = real * cosine - imag * sine
            moved_imag = real * sine + imag * cosine
            ins_ref[b] = jnp.concatenate(
                [moved_real * contrast, moved_imag * contrast], axis=1
            ).astype(jnp.bfloat16)
            right.append(
                jnp.concatenate([moved_real * scaled, moved_imag * scaled], axis=1).astype(
                    jnp.bfloat16
                )
            )
            start = pl.multiple_of((ROT - b) * owned, owned)
            left.append(turned[pl.ds(start, height), :])
        expo_ref[...] += lax.dot_general(
            jnp.concatenate(left, axis=1), jnp.concatenate(right, axis=1), by_lane,
            preferred_element_type=jnp.float32,
        )

    logp = expo_ref[...]
    peak = jnp.max(logp, axis=0, keepdims=True)
    expo = jnp.exp(logp - peak)
    expo_ref[...] = expo
    stat_ref[0] = jnp.broadcast_to(peak, (8, rows))
    stat_ref[1] = jnp.broadcast_to(jnp.sum(expo, axis=0, keepdims=True), (8, rows))


def insert_kernel(
    stat_ref, expo_ref, ins_ref, square_ref, inv_tau_ref, fresh_ref, weight_ref, loglik_ref, turned
):
    rows = expo_ref.shape[1]
    height = expo_ref.shape[0]
    owned = height // ROT
    count = rows // TRANS
    peaks, sums = stat_ref[0], stat_ref[1]
    peak = jnp.broadcast_to(jnp.max(peaks, axis=0, keepdims=True), (8, rows))
    top = peak
    for t in range(1, TRANS):
        top = jnp.maximum(top, pltpu.roll(peak, t * count, 1))
    part = jnp.sum(sums * jnp.exp(peaks - top[:1]), axis=0, keepdims=True)
    part = jnp.broadcast_to(part, (8, rows))
    total = part
    for t in range(1, TRANS):
        total = total + pltpu.roll(part, t * count, 1)
    loglik_ref[...] = top + jnp.log(total)
    factor = jnp.exp(stat_ref[2][:1] - top[:1]) / total[:1]

    summed = jnp.zeros((owned, rows), jnp.float32)
    for r in range(ROT):
        post = (expo_ref[r * owned : (r + 1) * owned] * factor).astype(jnp.bfloat16)
        summed = summed + post.astype(jnp.float32)
        first = (ROT - r) % ROT
        for spot in (first, first + ROT):
            turned[spot * owned : (spot + 1) * owned] = post
    weight_ref[...] = jnp.broadcast_to(jnp.sum(summed, axis=1, keepdims=True), weight_ref.shape)
    denom = jnp.dot(summed, square_ref[...], precision=HIGH, preferred_element_type=jnp.float32)
    inverse = 1.0 / (denom + inv_tau_ref[...])
    inverse = jnp.concatenate([inverse, inverse], axis=1)

    fresh_ref[...] = jnp.zeros_like(fresh_ref)

    @pl.loop(0, ROT // BATCH)
    def _(batch):
        left, right = [], []
        for part_index in range(BATCH):
            s = batch * BATCH + part_index
            start = pl.multiple_of((ROT - s) * owned, owned)
            left.append(turned[pl.ds(start, height), :])
            right.append(ins_ref[s])
        fresh_ref[...] += jnp.dot(
            jnp.concatenate(left, axis=1), jnp.concatenate(right, axis=0),
            preferred_element_type=jnp.float32,
        )

    for b in range(ROT):
        block = pl.ds(b * owned, owned)
        fresh_ref[block] = fresh_ref[block] * inverse


def per_device(
    images, references, class_logprior, ctf_table, noise_power, tau_power, defocus, offsets
):
    n = lax.axis_size("img")
    local = images.shape[0]
    count = local * n
    rows = count * TRANS
    owned_true = references.shape[0]
    owned = -(-owned_true // 16) * 16
    spare = owned - owned_true
    vmem = pl.BlockSpec(memory_space=pltpu.VMEM)
    limit = 60 * 1024 * 1024

    moves = offsets.astype(jnp.float32)
    meta = jnp.concatenate(
        [defocus.astype(jnp.float32)[:, None], moves[..., 0], moves[..., 1]], axis=1
    )
    meta = jnp.pad(meta, ((0, 0), (0, LANES - meta.shape[1]))).astype(jnp.bfloat16)
    own = jnp.concatenate([turn_major(images), meta[None]], axis=0)
    gathered = gather_images(own, n)
    refs = jnp.pad(turn_major(references), ((0, 0), (0, spare), (0, 0)))
    prior = jnp.pad(class_logprior.astype(jnp.float32), (0, spare), constant_values=-1e30)
    prior = jnp.broadcast_to(prior[:, None], (owned, 128))

    inserted, expo, stat, square = pl.pallas_call(
        score_kernel,
        out_shape=(
            jax.ShapeDtypeStruct((ROT, rows, LANES), jnp.bfloat16),
            jax.ShapeDtypeStruct((ROT * owned, rows), jnp.float32),
            jax.ShapeDtypeStruct((2, 8, rows), jnp.float32),
            jax.ShapeDtypeStruct((rows, HALF), jnp.float32),
        ),
        in_specs=[vmem] * 6,
        out_specs=(vmem,) * 4,
        scratch_shapes=[pltpu.VMEM((2 * ROT * owned, LANES), jnp.bfloat16)],
        compiler_params=pltpu.CompilerParams(vmem_limit_bytes=limit),
        name="score",
    )(
        gathered,
        refs,
        prior,
        jnp.tile(ctf_table, (1, STRIDE)),
        jnp.tile(noise_power, STRIDE)[None],
        jnp.asarray(phase_rows()),
    )
    every = lax.all_gather(stat[:, 0], ("img", "cls"), axis=1)
    stats = jnp.concatenate(
        [every, jnp.broadcast_to(stat[:1, :1], (1,) + every.shape[1:])], axis=0
    )
    fresh, weight, loglik = pl.pallas_call(
        insert_kernel,
        out_shape=(
            jax.ShapeDtypeStruct((ROT * owned, LANES), jnp.float32),
            jax.ShapeDtypeStruct((owned, 128), jnp.float32),
            jax.ShapeDtypeStruct((8, rows), jnp.float32),
        ),
        in_specs=[vmem] * 5,
        out_specs=(vmem,) * 3,
        scratch_shapes=[pltpu.VMEM((2 * ROT * owned, rows), jnp.bfloat16)],
        compiler_params=pltpu.CompilerParams(vmem_limit_bytes=limit),
        name="insert",
    )(stats, expo, inserted, square, jnp.tile(1.0 / tau_power, STRIDE)[None])
    fresh = fresh.reshape(ROT, owned, 2, STRIDE, CYCLES)[:, :owned_true]
    fresh = fresh.transpose(1, 2, 4, 0, 3).reshape(owned_true, 2 * CYCLES * ANG)
    mine = lax.dynamic_slice_in_dim(loglik[0], lax.axis_index("img") * local, local, 0)
    return fresh, weight[:owned_true, 0] / count, mine


def solution(mesh):
    return jax.shard_map(
        per_device,
        mesh=mesh,
        in_specs=(
            P("img", None),
            P(("img", "cls"), None),
            P(("img", "cls")),
            P(),
            P(),
            P(),
            P("img"),
            P("img", None, None),
        ),
        out_specs=(P(("img", "cls"), None), P(("img", "cls")), P("img")),
        check_vma=False,
    )
```

time: 557 us -> 139 us (0.25)
  other arithmetic: 186 us -> 4.72 us
  local copies, waits for them, and re-layouts: 182 us -> 30 us
  matrix products: 78.1 us -> 0 us
  waiting for transfers between devices: 44.1 us -> 0 us
  Pallas kernels: 0 us -> 34.5 us
  blocking collectives: 47.4 us -> 68.9 us
  between operations: 15.2 us -> 0.72 us
    concatenate x9 -> x2, other arithmetic: 91.8 us -> 1.31 us  [the longest x1 0.68 us: per_device(): own = jnp.concatenate([turn_major(images), meta[None]], axis=0)]
    another operation x36 -> x6, local copies, waits for them, and re-layouts: 90 us -> 3.22 us  [the longest x2 1.38 us: per_device(): jnp.tile(ctf_table, (1, STRIDE))]
    dot_general x21 -> x0, matrix products: 78.1 us -> none  [the longest x9 45.7 us: insert_group(): lax.dot_general(section, rotated, (((0,), (0,)), ((), ())), preferred_ele...]
    another operation x18 -> x1, other arithmetic: 73.5 us -> 0.69 us  [turned_rows(): jnp.stack(turned, axis=1)]
    all_gather x0 -> x1, blocking collectives: none -> 68.9 us  [per_device(): every = lax.all_gather(stat[:, 0], ('img', 'cls'), axis=1)]
    reshape x10 -> x3, local copies, waits for them, and re-layouts: 67.7 us -> 4.15 us  [the longest x1 2.21 us: per_device(): fresh = fresh.reshape(ROT, owned, 2, STRIDE, CYCLES)[:, :owned_true]]
    reduce_scatter x2 -> x0, waiting for transfers between devices: 37.4 us -> none  [the longest x1 37.4 us: per_device(): lax.psum_scatter(numer, 'img', scatter_dimension=0, tiled=True)]
    pallas_call x0 -> x3, Pallas kernels: none -> 34.5 us  [the longest x1 14.7 us: gather_images(): pl.pallas_call(lambda *refs: gather_kernel(n, *refs), out_shape=jax.Shape...]
  transfers between devices with their start and end apart: 3 -> 0, of which waited for: 2 -> 0; matrix products, arithmetic and copies ran while one was open for 37% -> 0% of each run, Pallas kernels for 0% -> 0%
where the time goes in v1:
time: 139 us
  blocking collectives  68.9 us (50%)
  Pallas kernels  34.5 us (25%)
  local copies, waits for them, and re-layouts  30 us (22%)
  other arithmetic  4.72 us (3%)
    all_gather x1, blocking collectives, per_device(): every = lax.all_gather(stat[:, 0], ('img', 'cls'), axis=1)  68.9 us
    pallas_call x1, Pallas kernels, gather_images(): pl.pallas_call(lambda *refs: gather_kernel(n, *refs), out_shape=jax.Shape...  14.7 us
    pallas_call x1, Pallas kernels, per_device(): pl.pallas_call(score_kernel, out_shape=(jax.ShapeDtypeStruct((ROT, rows,...  11.6 us
    pallas_call x1, Pallas kernels, per_device(): pl.pallas_call(insert_kernel, out_shape=(jax.ShapeDtypeStruct((ROT * owne...  8.21 us
    unnamed x5, local copies, waits for them, and re-layouts  6.82 us
    transpose x2, local copies, waits for them, and re-layouts, turn_major(): return shaped.transpose(3, 0, 1, 4, 2).reshape(ROT, source.shape[0], LANES)  5.88 us
    transpose x1, local copies, waits for them, and re-layouts, per_device(): fresh = fresh.transpose(1, 2, 4, 0, 3).reshape(owned_true, 2 * CYCLES * ANG)  5.61 us

profile of v1, /device:TPU:0, one launch (start us, length us, event | category | flops | bytes accessed | tf_op | source)
XLA Modules:
  0.0 138.9 jit_solution(13920122297193235385)
XLA Ops:
  0.6 0.7 broadcast_divide_fusion
  1.3 0.7 convert_bitcast_fusion
  2.0 0.1 copy.29
  2.1 0.6 broadcast_in_dim_tile.7.inv_tau_ref
  2.7 0.7 tile.10
  3.3 0.6 broadcast_in_dim_tile.6.noise_ref
  3.9 0.7 convert_convert_fusion
  4.6 0.1 copy.38
  4.7 0.1 copy.39
  4.8 0.1 fusion.5
  4.9 1.3 broadcast_in_dim.22.prior_ref
  6.2 0.7 tile.8
  6.9 0.7 tile.9.ctf_ref
  7.6 2.0 %copy.27 = bf16[8,9216]{0,1:T(8,128)(2,1)S(1)} copy(bf16[8,9216]{1,0:T(8,128)(2,1)} %param.9) | data formatting | bytes 294912 | tf_op args[0]
  9.5 0.0 copy-start
  9.5 1.3 copy.28
  10.9 0.4 reshape.37
  11.3 0.7 pad_maximum_fusion.refs_0_
  12.0 14.7 %gather_images.1.images_ref = bf16[8,37,8,256]{3,2,1,0:T(8,128)(2,1)} custom-call(bf16[37,8,256]{2,1,0:T(8,128)(2,1)} %pad_maximum_fusion.refs_0_), custom_call_target="tpu_custom_call" | custom-call | tf_op jit(solution)/shard_map/gather_images/pallas_call | solution.py:97
  26.7 0.0 copy-done
  26.7 1.1 copy.32
  27.8 4.5 %copy.33 = bf16[36,16,2,4,32]{4,3,2,1,0:T(4,128)(2,1)S(1)} copy(bf16[36,16,2,4,32]{1,3,0,4,2:T(4,128)(2,1)S(1)} %bitcast.20) | data formatting | bytes 589824 | tf_op jit(solution)/shard_map/transpose | solution.py:51
  32.4 1.6 %reshape.39.refs_ref = bf16[36,16,256]{2,1,0:T(8,128)(2,1)} reshape(bf16[36,16,2,4,32]{4,3,2,1,0:T(4,128)(2,1)S(1)} %copy.33) | data formatting | bytes 589824 | tf_op jit(solution)/shard_map/reshape | solution.py:51
  33.9 11.6 %score.1 = (bf16[36,256,256]{2,1,0:T(8,128)(2,1)}, f32[576,256]{1,0:T(8,128)}, f32[2,8,256]{2,1,0:T(8,128)}, f32[256,128]{1,0:T(8,128)}) custom-call(bf16[8,37,8,256]{3,2,1,0:T(8,128)(2,1)} %gather_images.1.images_ref, bf16[36,16,256]{2,1,0:T(8,128)(2,1)} %reshape.39.refs_ref, f32[16,128]{1,0:T(8,128)} %broadcast_in_dim.22.prior_ref, ...), custom_call_target="tpu_custom_call" | custom-call | tf_op jit(solution)/shard_map/score/pallas_call | solution.py:275
  45.6 0.7 slice.23
  46.3 0.7 slice.22
  47.0 68.9 %all_gather.3 = f32[2,32,256]{2,0,1:T(2,128)S(1)} all-gather(f32[2,1,256]{2,0,1:T(2,128)S(1)} %copy.34), channel_id=1, replica_groups=mesh['img'=8,'cls'=4] {'img','cls'}, dimensions={1}, use_global_device_ids=true | all-gather | bytes 67584 | tf_op jit(solution)/shard_map/all_gather | solution.py:296
  115.9 0.6 pad_maximum_fusion.1.stat_ref
  116.6 8.2 %insert.1 = (f32[576,256]{1,0:T(8,128)}, f32[16,128]{1,0:T(8,128)}, f32[8,256]{1,0:T(8,128)}) custom-call(f32[3,32,256]{2,1,0:T(8,128)} %pad_maximum_fusion.1.stat_ref, f32[576,256]{1,0:T(8,128)} %get-tuple-element.11.expo_ref, bf16[36,256,256]{2,1,0:T(8,128)(2,1)} %get-tuple-element.12.ins_ref, f32[256,128]{1,0:T(8,128)} %get-tuple-element.13.square_ref, ...), custom_call_target="tpu_custom_call" | custom-call | tf_op jit(solution)/shard_map/insert/pallas_call | solution.py:300
  124.8 1.3 multiply_reduce_fusion
  126.1 0.7 slice.25
  126.8 0.6 dynamic-slice_bitcast_fusion
  127.4 2.2 %reshape.40 = f32[36,16,2,4,32]{4,3,2,1,0:T(4,128)S(1)} reshape(f32[576,256]{1,0:T(8,128)} %get-tuple-element.14) | data formatting | bytes 1179648 | tf_op jit(solution)/shard_map/reshape | solution.py:313
  129.6 5.6 %copy.36 = f32[16,2,32,36,4]{0,4,3,2,1:T(4,128)} copy(f32[16,2,32,36,4]{2,4,1,0,3:T(4,128)S(1)} %bitcast.18) | data formatting | bytes 1179648 | tf_op jit(solution)/shard_map/transpose | solution.py:314
  135.2 3.7 %copy.37 = f32[16,9216]{1,0:T(8,128)} copy(f32[16,9216]{0,1:T(8,128)} %bitcast.17) | data formatting | bytes 1179648
  (5 shorter events, 0.0 us)
Async XLA Ops:
  9.5 17.2 %copy-start = (bf16[16,9216]{1,0:T(8,128)(2,1)S(1)}, bf16[16,9216]{1,0:T(8,128)(2,1)}, u32[]{:S(2)}) copy-start(bf16[16,9216]{1,0:T(8,128)(2,1)} %param.10) | copy-start | bytes 884740

commit v2 on v1

--- a/solution.py
+++ b/solution.py
@@ -107,6 +107,63 @@
         ],
         compiler_params=pltpu.CompilerParams(collective_id=0, has_side_effects=True),
         name="gather_images",
+    )(own)
+
+
+def exchange_kernel(n, m, own_ref, all_ref, local_sem, cls_send, cls_recv, img_send, img_recv):
+    row, column = lax.axis_index("img"), lax.axis_index("cls")
+    above = [{"cls": lax.rem(column + hop, m)} for hop in range(1, m)]
+    beside = [{"img": lax.rem(row + hop, n)} for hop in range(1, n)]
+    barrier = pltpu.get_barrier_semaphore()
+    for peer in above + beside:
+        pl.semaphore_signal(barrier, inc=1, device_id=peer, device_id_type=pl.DeviceIdType.MESH)
+    pl.semaphore_wait(barrier, n + m - 2)
+
+    def send_all(src, dst, peers, left, landed):
+        copies = []
+        for hop, peer in enumerate(peers):
+            copy = pltpu.make_async_remote_copy(
+                src_ref=src,
+                dst_ref=dst,
+                send_sem=left.at[hop],
+                recv_sem=landed.at[hop],
+                device_id=peer,
+                device_id_type=pl.DeviceIdType.MESH,
+            )
+            copy.start()
+            copies.append(copy)
+        return copies
+
+    slot = all_ref.at[row, column]
+    first = send_all(own_ref, slot, above, cls_send, cls_recv)
+    keep = pltpu.make_async_copy(own_ref, slot, local_sem)
+    keep.start()
+    keep.wait()
+    for copy in first:
+        copy.wait_recv()
+    second = send_all(all_ref.at[row], all_ref.at[row], beside, img_send, img_recv)
+    for copy in second:
+        copy.wait_recv()
+    for copy in first + second:
+        copy.wait_send()
+
+
+def exchange_stats(own, n, m):
+    vmem = pl.BlockSpec(memory_space=pltpu.VMEM)
+    return pl.pallas_call(
+        lambda *refs: exchange_kernel(n, m, *refs),
+        out_shape=jax.ShapeDtypeStruct((n, m) + own.shape, own.dtype),
+        in_specs=[vmem],
+        out_specs=vmem,
+        scratch_shapes=[
+            pltpu.SemaphoreType.DMA,
+            pltpu.SemaphoreType.DMA((m,)),
+            pltpu.SemaphoreType.DMA((m,)),
+            pltpu.SemaphoreType.DMA((n,)),
+            pltpu.SemaphoreType.DMA((n,)),
+        ],
+        compiler_params=pltpu.CompilerParams(collective_id=1, has_side_effects=True),
+        name="exchange_stats",
     )(own)
 
 
@@ -192,18 +249,18 @@
     peak = jnp.max(logp, axis=0, keepdims=True)
     expo = jnp.exp(logp - peak)
     expo_ref[...] = expo
-    stat_ref[0] = jnp.broadcast_to(peak, (8, rows))
-    stat_ref[1] = jnp.broadcast_to(jnp.sum(expo, axis=0, keepdims=True), (8, rows))
+    which = lax.broadcasted_iota(jnp.int32, (8, rows), 0)
+    stat_ref[...] = jnp.where(which == 0, peak, jnp.sum(expo, axis=0, keepdims=True))
 
 
 def insert_kernel(
-    stat_ref, expo_ref, ins_ref, square_ref, inv_tau_ref, fresh_ref, weight_ref, loglik_ref, turned
+    every_ref, stat_ref, expo_ref, ins_ref, square_ref, inv_tau_ref, fresh_ref, weight_ref, loglik_ref, turned
 ):
     rows = expo_ref.shape[1]
     height = expo_ref.shape[0]
     owned = height // ROT
     count = rows // TRANS
-    peaks, sums = stat_ref[0], stat_ref[1]
+    peaks, sums = every_ref[:, 0, :], every_ref[:, 1, :]
     peak = jnp.broadcast_to(jnp.max(peaks, axis=0, keepdims=True), (8, rows))
     top = peak
     for t in range(1, TRANS):
@@ -214,7 +271,7 @@
     for t in range(1, TRANS):
         total = total + pltpu.roll(part, t * count, 1)
     loglik_ref[...] = top + jnp.log(total)
-    factor = jnp.exp(stat_ref[2][:1] - top[:1]) / total[:1]
+    factor = jnp.exp(stat_ref[:1] - top[:1]) / total[:1]
 
     summed = jnp.zeros((owned, rows), jnp.float32)
     for r in range(ROT):
@@ -277,7 +334,7 @@
         out_shape=(
             jax.ShapeDtypeStruct((ROT, rows, LANES), jnp.bfloat16),
             jax.ShapeDtypeStruct((ROT * owned, rows), jnp.float32),
-            jax.ShapeDtypeStruct((2, 8, rows), jnp.float32),
+            jax.ShapeDtypeStruct((8, rows), jnp.float32),
             jax.ShapeDtypeStruct((rows, HALF), jnp.float32),
         ),
         in_specs=[vmem] * 6,
@@ -293,10 +350,7 @@
         jnp.tile(noise_power, STRIDE)[None],
         jnp.asarray(phase_rows()),
     )
-    every = lax.all_gather(stat[:, 0], ("img", "cls"), axis=1)
-    stats = jnp.concatenate(
-        [every, jnp.broadcast_to(stat[:1, :1], (1,) + every.shape[1:])], axis=0
-    )
+    every = exchange_stats(stat, n, lax.axis_size("cls")).reshape(-1, 8, rows)
     fresh, weight, loglik = pl.pallas_call(
         insert_kernel,
         out_shape=(
@@ -304,12 +358,12 @@
             jax.ShapeDtypeStruct((owned, 128), jnp.float32),
             jax.ShapeDtypeStruct((8, rows), jnp.float32),
         ),
-        in_specs=[vmem] * 5,
+        in_specs=[vmem] * 6,
         out_specs=(vmem,) * 3,
         scratch_shapes=[pltpu.VMEM((2 * ROT * owned, rows), jnp.bfloat16)],
         compiler_params=pltpu.CompilerParams(vmem_limit_bytes=limit),
         name="insert",
-    )(stats, expo, inserted, square, jnp.tile(1.0 / tau_power, STRIDE)[None])
+    )(every, stat, expo, inserted, square, jnp.tile(1.0 / tau_power, STRIDE)[None])
     fresh = fresh.reshape(ROT, owned, 2, STRIDE, CYCLES)[:, :owned_true]
     fresh = fresh.transpose(1, 2, 4, 0, 3).reshape(owned_true, 2 * CYCLES * ANG)
     mine = lax.dynamic_slice_in_dim(loglik[0], lax.axis_index("img") * local, local, 0)

time: 139 us -> 80.9 us (0.58)
  blocking collectives: 68.9 us -> 0 us
  Pallas kernels: 34.5 us -> 47 us
  local copies, waits for them, and re-layouts: 30 us -> 28.6 us
    all_gather x1 -> x0, blocking collectives: 68.9 us -> none  [per_device(): every = lax.all_gather(stat[:, 0], ('img', 'cls'), axis=1)]
    pallas_call x0 -> x1, Pallas kernels: none -> 12.4 us  [exchange_stats(): pl.pallas_call(lambda *refs: exchange_kernel(n, m, *refs), out_shape=jax....]
    slice x3 -> x0, local copies, waits for them, and re-layouts: 1.42 us -> none  [the longest x2 0.72 us: per_device(): every = lax.all_gather(stat[:, 0], ('img', 'cls'), axis=1)]
where the time goes in v2:
time: 80.9 us; the launch traced here: 80.4 us
  Pallas kernels  47 us (58%)
  local copies, waits for them, and re-layouts  28.6 us (35%)
  other arithmetic  4.09 us (5%)
    pallas_call x1, Pallas kernels, gather_images(): pl.pallas_call(lambda *refs: gather_kernel(n, *refs), out_shape=jax.Shape...  14.7 us
    pallas_call x1, Pallas kernels, exchange_stats(): pl.pallas_call(lambda *refs: exchange_kernel(n, m, *refs), out_shape=jax....  12.4 us
    pallas_call x1, Pallas kernels, per_device(): pl.pallas_call(score_kernel, out_shape=(jax.ShapeDtypeStruct((ROT, rows,...  11.6 us
    pallas_call x1, Pallas kernels, per_device(): pl.pallas_call(insert_kernel, out_shape=(jax.ShapeDtypeStruct((ROT * owne...  8.29 us
    unnamed x5, local copies, waits for them, and re-layouts  6.82 us
    transpose x2, local copies, waits for them, and re-layouts, turn_major(): return shaped.transpose(3, 0, 1, 4, 2).reshape(ROT, source.shape[0], LANES)  5.88 us
    transpose x1, local copies, waits for them, and re-layouts, per_device(): fresh = fresh.transpose(1, 2, 4, 0, 3).reshape(owned_true, 2 * CYCLES * ANG)  5.61 us
    reshape x1, local copies, waits for them, and re-layouts, per_device(): fresh = fresh.reshape(ROT, owned, 2, STRIDE, CYCLES)[:, :owned_true]  2.21 us

profile of v2, /device:TPU:0, one launch (start us, length us, event | category | flops | bytes accessed | tf_op | source)
XLA Modules:
  0.0 80.4 jit_solution(10324528847084417270)
XLA Ops:
  0.6 0.7 broadcast_divide_fusion
  1.3 0.7 convert_bitcast_fusion
  2.0 0.1 copy.20
  2.1 0.6 broadcast_in_dim_tile.7.inv_tau_ref
  2.7 0.7 tile.10
  3.3 0.6 broadcast_in_dim_tile.6.noise_ref
  3.9 0.7 convert_convert_fusion
  4.6 0.1 copy.27
  4.7 0.1 copy.28
  4.8 0.1 fusion.5
  4.9 1.3 %broadcast_in_dim.15.prior_ref = f32[16,128]{1,0:T(8,128)} broadcast(bf16[16]{0:T(256)(128)(2,1)} %param.11), dimensions={0} | broadcast | bytes 8224 | tf_op jit(solution)/shard_map/broadcast_in_dim | solution.py:330
  6.2 0.7 tile.8
  6.9 0.7 tile.9.ctf_ref
  7.6 2.0 %copy.18 = bf16[8,9216]{0,1:T(8,128)(2,1)S(1)} copy(bf16[8,9216]{1,0:T(8,128)(2,1)} %param.9) | data formatting | bytes 294912 | tf_op args[0]
  9.5 0.0 copy-start
  9.5 1.3 %copy.19 = bf16[36,8,2,4,32]{4,3,2,1,0:T(4,128)(2,1)S(1)} copy(bf16[36,8,2,4,32]{1,3,0,4,2:T(4,128)(2,1)S(1)} %bitcast.19) | data formatting | bytes 294912 | tf_op jit(solution)/shard_map/transpose | solution.py:51
  10.9 0.4 reshape.38
  11.3 0.7 pad_maximum_fusion.refs_0_
  12.0 14.7 %gather_images.1.images_ref = bf16[8,37,8,256]{3,2,1,0:T(8,128)(2,1)} custom-call(bf16[37,8,256]{2,1,0:T(8,128)(2,1)} %pad_maximum_fusion.refs_0_), custom_call_target="tpu_custom_call" | custom-call | tf_op jit(solution)/shard_map/gather_images/pallas_call | solution.py:97
  26.7 0.0 copy-done
  26.7 1.1 %copy.23 = bf16[16,9216]{0,1:T(8,128)(2,1)S(1)} copy(bf16[16,9216]{1,0:T(8,128)(2,1)S(1)} %copy-done) | data formatting | bytes 589824 | tf_op args[1]
  27.8 4.5 %copy.24 = bf16[36,16,2,4,32]{4,3,2,1,0:T(4,128)(2,1)S(1)} copy(bf16[36,16,2,4,32]{1,3,0,4,2:T(4,128)(2,1)S(1)} %bitcast.20) | data formatting | bytes 589824 | tf_op jit(solution)/shard_map/transpose | solution.py:51
  32.4 1.6 %reshape.40.refs_ref = bf16[36,16,256]{2,1,0:T(8,128)(2,1)} reshape(bf16[36,16,2,4,32]{4,3,2,1,0:T(4,128)(2,1)S(1)} %copy.24) | data formatting | bytes 589824 | tf_op jit(solution)/shard_map/reshape | solution.py:51
  33.9 11.6 %score.1 = (bf16[36,256,256]{2,1,0:T(8,128)(2,1)}, f32[576,256]{1,0:T(8,128)}, f32[8,256]{1,0:T(8,128)}, f32[256,128]{1,0:T(8,128)}) custom-call(bf16[8,37,8,256]{3,2,1,0:T(8,128)(2,1)} %gather_images.1.images_ref, bf16[36,16,256]{2,1,0:T(8,128)(2,1)} %reshape.40.refs_ref, f32[16,128]{1,0:T(8,128)} %broadcast_in_dim.15.prior_ref, f32[16,128]{1,0:T(8,128)} %tile.9.ctf_ref, ...), custom_call_target="tpu_custom_call" | custom-call | tf_op jit(solution)/shard_map/score/pallas_call | solution.py:332
  45.6 12.4 %exchange_stats.1 = f32[8,4,8,256]{3,2,1,0:T(8,128)} custom-call(f32[8,256]{1,0:T(8,128)} %get-tuple-element.10.refs_0_.stat_ref), custom_call_target="tpu_custom_call" | custom-call | tf_op jit(solution)/shard_map/exchange_stats/pallas_call | solution.py:153
  58.0 8.3 %insert.1 = (f32[576,256]{1,0:T(8,128)}, f32[16,128]{1,0:T(8,128)}, f32[8,256]{1,0:T(8,128)}) custom-call(f32[32,8,256]{2,1,0:T(8,128)} %bitcast.21, f32[8,256]{1,0:T(8,128)} %get-tuple-element.10.refs_0_.stat_ref, f32[576,256]{1,0:T(8,128)} %get-tuple-element.11.expo_ref, bf16[36,256,256]{2,1,0:T(8,128)(2,1)} %get-tuple-element.12.ins_ref, ...), custom_call_target="tpu_custom_call" | custom-call | tf_op jit(solution)/shard_map/insert/pallas_call | solution.py:354
  66.2 1.3 %multiply_reduce_fusion = f32[16]{0:T(128)} fusion(f32[16,128]{1,0:T(8,128)} %get-tuple-element.15), kind=kLoop, calls=%fused_computation.5 | loop fusion | flops 16 | bytes 128 | tf_op jit(solution)/shard_map/div | solution.py:370
  67.6 0.7 slice.17
  68.3 0.6 dynamic-slice_bitcast_fusion
  68.8 2.2 %reshape.42 = f32[36,16,2,4,32]{4,3,2,1,0:T(4,128)S(1)} reshape(f32[576,256]{1,0:T(8,128)} %get-tuple-element.14) | data formatting | bytes 1179648 | tf_op jit(solution)/shard_map/reshape | solution.py:367
  71.1 5.6 %copy.25 = f32[16,2,32,36,4]{0,4,3,2,1:T(4,128)} copy(f32[16,2,32,36,4]{2,4,1,0,3:T(4,128)S(1)} %bitcast.18) | data formatting | bytes 1179648 | tf_op jit(solution)/shard_map/transpose | solution.py:368
  76.7 3.7 %copy.26 = f32[16,9216]{1,0:T(8,128)} copy(f32[16,9216]{0,1:T(8,128)} %bitcast.17) | data formatting | bytes 1179648
  (2 shorter events, 0.0 us)
Async XLA Ops:
  9.5 17.2 %copy-start = (bf16[16,9216]{1,0:T(8,128)(2,1)S(1)}, bf16[16,9216]{1,0:T(8,128)(2,1)}, u32[]{:S(2)}) copy-start(bf16[16,9216]{1,0:T(8,128)(2,1)} %param.10) | copy-start | bytes 884740
